TPU v7x, 32 devices: a whole 2x2x4 slice. The times are simulated.
32 devices in a mesh: seq: 16 (over z, y, x), head: 2 (over core).
Axes of the slice: x: 2, y: 2, z: 4, core: 2. Of those that a mesh axis runs over, the one named last changes fastest.
Arguments:
- win_query: bfloat16 [4096, 4096], P('seq', 'head'), may hold values from -24 to 24
- win_key: bfloat16 [4096, 4096], P('seq', 'head'), may hold values from -24 to 24
- win_value: bfloat16 [4096, 4096], P('seq', 'head'), may hold values from -24 to 24
- clu_query: bfloat16 [4096, 4096], P('seq', 'head'), may hold values from -24 to 24
- clu_key: bfloat16 [4096, 4096], P('seq', 'head'), may hold values from -24 to 24
- clu_value: bfloat16 [4096, 4096], P('seq', 'head'), may hold values from -24 to 24
- cluster_ids: int32 [32, 4096], P('head', 'seq'), may hold values from 0 to 63, as said below
- win_gain: float32 [4096], P('head'), may hold values from 0.5 to 1.5
- clu_gain: float32 [4096], P('head'), may hold values from 0.5 to 1.5
- win_out_grad: bfloat16 [4096, 4096], P('seq', 'head'), may hold values from -9 to 9
- clu_out_grad: bfloat16 [4096, 4096], P('seq', 'head'), may hold values from -9 to 9
Outputs:
- win_normed: bfloat16 [4096, 4096], P('seq', 'head')
- clu_normed: bfloat16 [4096, 4096], P('seq', 'head')
- win_dq: bfloat16 [4096, 4096], P('seq', 'head')
- win_dk: bfloat16 [4096, 4096], P('seq', 'head')
- win_dv: bfloat16 [4096, 4096], P('seq', 'head')
- clu_dq: bfloat16 [4096, 4096], P('seq', 'head')
- clu_dk: bfloat16 [4096, 4096], P('seq', 'head')
- clu_dv: bfloat16 [4096, 4096], P('seq', 'head')
Inputs may be any that keep to these rules, and one draw needn't show every extreme that they name: `cluster_ids`: in every cluster head each cluster holds at most 8 of the tokens of each aligned block of 256 positions, hence at most 128 tokens in all; in every head one cluster holds exactly 8 tokens of every block.
All inputs are finite; a program needn't handle non-finite values.
Results may differ from a plain program's by a relative error of at most 0.035.
Values may be sent and summed in bfloat16 or wider, within the bound.
A program may use at most 192 MiB of HBM per device.

v0:
```python
import jax
import jax.numpy as jnp
from jax import lax
from jax.sharding import PartitionSpec as P

HW = 32
HC = 32
DH = 128
WINDOW = 256
SLOTS = 128
EPSILON = 1e-06


def from_behind(block, axis, distance):
    devices = range(lax.axis_size(axis))
    route = [(i - distance, i) for i in devices if i - distance in devices]
    return lax.ppermute(block, axis, route)


def split_heads(values):
    return values.reshape(values.shape[0], values.shape[1] // DH, DH)


def five_dims(values):
    return values.reshape(
        values.shape[0], values.shape[1], values.shape[2], values.shape[3] // DH, DH
    )


def softmax_rows(scores, allowed):
    masked = jnp.where(allowed, scores, -jnp.inf)
    top_row = jnp.max(masked, axis=-1, keepdims=True)
    summed = jnp.sum(jnp.exp(masked - top_row), axis=-1, keepdims=True)
    return jnp.exp(masked - (top_row + jnp.log(summed)))


def owner_attend(queries, key_rows, val_rows, filled, factor):
    layout = queries.shape
    sources, n_items, n_cap, n_heads = (layout[0], layout[1], layout[2], layout[3])
    member_count = sources * n_cap
    scores = jnp.einsum(
        "scahd,tcbhd->hcsatb", queries, key_rows, preferred_element_type=jnp.float32
    )
    scores = scores.reshape(n_heads, n_items, member_count, member_count) * factor
    live_cols = filled.transpose(3, 1, 0, 2).reshape(n_heads, n_items, 1, member_count) > 0
    row_pos = lax.broadcasted_iota(jnp.int32, (member_count, member_count), 0)
    col_pos = lax.broadcasted_iota(jnp.int32, (member_count, member_count), 1)
    allowed = live_cols & (col_pos <= row_pos) | (col_pos == row_pos)
    attn_prob = softmax_rows(scores, allowed)
    weights = attn_prob.astype(jnp.bfloat16)
    six_dims = (n_heads, n_items, sources, n_cap, sources, n_cap)
    outputs = jnp.einsum(
        "hcsatb,tcbhd->scahd",
        weights.reshape(six_dims),
        val_rows,
        preferred_element_type=jnp.float32,
    ).astype(jnp.bfloat16)
    return (attn_prob, weights, outputs)


def owner_gradients(queries, key_rows, val_rows, attn_prob, weights, outputs, grad_rows, factor):
    layout = queries.shape
    sources, n_items, n_cap, n_heads = (layout[0], layout[1], layout[2], layout[3])
    member_count = sources * n_cap
    six_dims = (n_heads, n_items, sources, n_cap, sources, n_cap)
    flat_dims = (sources, n_items, n_cap, n_heads * DH)
    row_dot = jnp.sum(grad_rows.astype(jnp.float32) * outputs.astype(jnp.float32), axis=-1)
    row_dot = row_dot.transpose(3, 1, 0, 2).reshape(n_heads, n_items, member_count, 1)
    slope_rows = jnp.einsum(
        "scahd,tcbhd->hcsatb", grad_rows, val_rows, preferred_element_type=jnp.float32
    )
    slope_rows = slope_rows.reshape(n_heads, n_items, member_count, member_count)
    change = (attn_prob * (slope_rows - row_dot)).astype(jnp.bfloat16).reshape(six_dims)
    grad_q = jnp.einsum("hcsatb,tcbhd->scahd", change, key_rows, preferred_element_type=jnp.float32)
    grad_k = jnp.einsum("hcsatb,scahd->tcbhd", change, queries, preferred_element_type=jnp.float32)
    grad_v = jnp.einsum(
        "hcsatb,scahd->tcbhd",
        weights.reshape(six_dims),
        grad_rows,
        preferred_element_type=jnp.float32,
    )
    grad_q = (grad_q * factor).astype(jnp.bfloat16).reshape(flat_dims)
    grad_k = (grad_k * factor).astype(jnp.bfloat16).reshape(flat_dims)
    grad_v = grad_v.astype(jnp.bfloat16).reshape(flat_dims)
    return (grad_q, grad_k, grad_v)


def body(
    win_query,
    win_key,
    win_value,
    clu_query,
    clu_key,
    clu_value,
    cluster_ids,
    win_gain,
    clu_gain,
    win_out_grad,
    clu_out_grad,
):
    n_rows = win_query.shape[0]
    factor = DH ** (-0.5)
    feat_width = (HW + HC) * DH
    sources = lax.axis_size("seq")
    position = lax.axis_index("seq")
    n_cap = SLOTS // sources
    owned_count = 2 * n_rows // SLOTS
    pool_size = 2 * n_rows
    clu_heads = clu_query.shape[1] // DH
    rim_rows = jnp.stack([win_key, win_value])
    before = from_behind(rim_rows, "seq", 1)
    key_local = split_heads(jnp.concatenate([before[0], win_key], axis=0))
    val_local = split_heads(jnp.concatenate([before[1], win_value], axis=0))
    query_win = split_heads(win_query)
    row_pos = lax.broadcasted_iota(jnp.int32, (n_rows, n_rows + WINDOW), 0)
    col_pos = lax.broadcasted_iota(jnp.int32, (n_rows, n_rows + WINDOW), 1)
    gap_pos = row_pos + WINDOW - col_pos
    allowed = (gap_pos >= 0) & (gap_pos < WINDOW) & ((col_pos >= WINDOW) | (position > 0))
    scores = (
        jnp.einsum("ihd,jhd->hij", query_win, key_local, preferred_element_type=jnp.float32)
        * factor
    )
    prob_win = softmax_rows(scores, allowed)
    weight_win = prob_win.astype(jnp.bfloat16)
    attn_win = jnp.einsum(
        "hij,jhd->ihd", weight_win, val_local, preferred_element_type=jnp.float32
    ).astype(jnp.bfloat16)
    row_ids = lax.broadcasted_iota(jnp.int32, (n_rows, n_rows), 0)
    col_ids = lax.broadcasted_iota(jnp.int32, (n_rows, n_rows), 1)
    same_cluster = (cluster_ids[:, :, None] == cluster_ids[:, None, :]) & (col_ids < row_ids)
    rank_in = jnp.sum(same_cluster.astype(jnp.int32), axis=-1)
    slot_at = cluster_ids * n_cap + rank_in
    picker = (
        lax.broadcasted_iota(jnp.int32, (clu_heads, pool_size, n_rows), 1) == slot_at[:, None, :]
    ).astype(jnp.bfloat16)

    def dispatch(values):
        spread = jnp.einsum(
            "hpt,thd->phd", picker, split_heads(values), preferred_element_type=jnp.float32
        )
        return spread.astype(jnp.bfloat16).reshape(sources, owned_count, n_cap, clu_heads * DH)

    def collect(values):
        merged = jnp.einsum(
            "hpt,phd->thd",
            picker,
            values.reshape(pool_size, clu_heads, DH),
            preferred_element_type=jnp.float32,
        )
        return merged.astype(jnp.bfloat16).reshape(n_rows, clu_heads * DH)

    filled = jnp.sum(picker, axis=2).transpose(1, 0).reshape(sources, owned_count, n_cap, clu_heads)
    sent_query = dispatch(clu_query)
    sent_key = dispatch(clu_key)
    sent_value = dispatch(clu_value)
    queries = lax.all_to_all(sent_query, "seq", split_axis=0, concat_axis=0, tiled=True)
    key_rows = lax.all_to_all(sent_key, "seq", split_axis=0, concat_axis=0, tiled=True)
    val_rows = lax.all_to_all(sent_value, "seq", split_axis=0, concat_axis=0, tiled=True)
    live_rows = lax.all_to_all(filled, "seq", split_axis=0, concat_axis=0, tiled=True)
    q_five = five_dims(queries)
    k_five = five_dims(key_rows)
    v_five = five_dims(val_rows)
    attn_prob, weights, outputs = owner_attend(q_five, k_five, v_five, live_rows, factor)
    returned = lax.all_to_all(
        outputs.reshape(queries.shape), "seq", split_axis=0, concat_axis=0, tiled=True
    )
    result = (returned, q_five, k_five, v_five, attn_prob, weights, outputs)
    returned = result[0]
    attn_clu = collect(returned)
    flat_win = attn_win.reshape(n_rows, -1).astype(jnp.float32)
    flat_clu = attn_clu.astype(jnp.float32)
    sq_total = lax.psum(
        jnp.sum(flat_win * flat_win, axis=1) + jnp.sum(flat_clu * flat_clu, axis=1), "head"
    )
    inv_rms = 1.0 / jnp.sqrt(sq_total / feat_width + EPSILON)
    win_normed = (flat_win * inv_rms[:, None] * win_gain).astype(jnp.bfloat16)
    clu_normed = (flat_clu * inv_rms[:, None] * clu_gain).astype(jnp.bfloat16)
    grad_win = win_out_grad.astype(jnp.float32) * win_gain
    grad_clu = clu_out_grad.astype(jnp.float32) * clu_gain
    dot_total = lax.psum(
        jnp.sum(grad_win * flat_win, axis=1) + jnp.sum(grad_clu * flat_clu, axis=1), "head"
    )
    coef_rows = inv_rms**3 * dot_total / feat_width
    dout_win = (inv_rms[:, None] * grad_win - coef_rows[:, None] * flat_win).astype(jnp.bfloat16)
    dout_clu = (inv_rms[:, None] * grad_clu - coef_rows[:, None] * flat_clu).astype(jnp.bfloat16)
    dout_heads = split_heads(dout_win)
    row_dot_win = jnp.sum(dout_heads.astype(jnp.float32) * attn_win.astype(jnp.float32), axis=-1)
    slope_win = jnp.einsum(
        "ihd,jhd->hij", dout_heads, val_local, preferred_element_type=jnp.float32
    )
    change_win = (prob_win * (slope_win - row_dot_win.T[:, :, None])).astype(jnp.bfloat16)
    win_dq = jnp.einsum("hij,jhd->ihd", change_win, key_local, preferred_element_type=jnp.float32)
    win_dq = (win_dq * factor).astype(jnp.bfloat16).reshape(n_rows, -1)
    key_terms = jnp.einsum(
        "hij,ihd->jhd", change_win, query_win, preferred_element_type=jnp.float32
    )
    val_terms = jnp.einsum(
        "hij,ihd->jhd", weight_win, dout_heads, preferred_element_type=jnp.float32
    )
    rim_terms = jnp.stack([key_terms[:WINDOW], val_terms[:WINDOW]]).reshape(2, WINDOW, -1)
    after_rim = from_behind(rim_terms.astype(jnp.bfloat16), "seq", -1).astype(rim_terms.dtype)
    win_dk = key_terms[WINDOW:].reshape(n_rows, -1).at[n_rows - WINDOW :].add(after_rim[0])
    win_dk = (win_dk * factor).astype(jnp.bfloat16)
    win_dv = (
        val_terms[WINDOW:]
        .reshape(n_rows, -1)
        .at[n_rows - WINDOW :]
        .add(after_rim[1])
        .astype(jnp.bfloat16)
    )
    grad_sent = dispatch(dout_clu)
    grad_owned = lax.all_to_all(grad_sent, "seq", split_axis=0, concat_axis=0, tiled=True)
    grad_q, grad_k, grad_v = owner_gradients(
        result[1],
        result[2],
        result[3],
        result[4],
        result[5],
        result[6],
        five_dims(grad_owned),
        factor,
    )
    home_rows = (
        lax.all_to_all(grad_q, "seq", split_axis=0, concat_axis=0, tiled=True),
        lax.all_to_all(grad_k, "seq", split_axis=0, concat_axis=0, tiled=True),
        lax.all_to_all(grad_v, "seq", split_axis=0, concat_axis=0, tiled=True),
    )
    clu_dq = collect(home_rows[0])
    clu_dk = collect(home_rows[1])
    clu_dv = collect(home_rows[2])
    return (win_normed, clu_normed, win_dq, win_dk, win_dv, clu_dq, clu_dk, clu_dv)


def solution(mesh):
    return jax.shard_map(
        body,
        mesh=mesh,
        in_specs=(
            P("seq", "head"),
            P("seq", "head"),
            P("seq", "head"),
            P("seq", "head"),
            P("seq", "head"),
            P("seq", "head"),
            P("head", "seq"),
            P("head"),
            P("head"),
            P("seq", "head"),
            P("seq", "head"),
        ),
        out_specs=(
            P("seq", "head"),
            P("seq", "head"),
            P("seq", "head"),
            P("seq", "head"),
            P("seq", "head"),
            P("seq", "head"),
            P("seq", "head"),
            P("seq", "head"),
        ),
        check_vma=False,
    )
```

profile of v0, /device:TPU:14, one launch (start us, length us, event | category | flops | bytes accessed | tf_op | source)
XLA Modules:
  0.0 635.6 jit_solution(10428212256974955099)
XLA Ops:
  5.6 7.1 %all-to-all-start.1 = ((bf16[16,2,256]{2,1,0:T(2,128)(2,1)}), bf16[16,2,256]{2,1,0:T(2,128)(2,1)S(1)}, u32[]{:S(2)}, u32[]{:S(2)}) async-start(bf16[16,2,256]{2,1,0:T(2,128)(2,1)} %reshape.323), calls=%async_computation.1 | async-start | bytes 32768 | tf_op jit(solution)/shard_map/all_to_all | solution.py:159
  18.0 7.0 %all-to-all-start.3 = ((bf16[16,4,8,2048]{3,2,1,0:T(8,128)(2,1)}), bf16[16,4,8,2048]{3,2,1,0:T(8,128)(2,1)S(1)}, u32[]{:S(2)}, u32[]{:S(2)}) async-start(bf16[16,4,8,2048]{3,2,1,0:T(8,128)(2,1)} %reshape.287), calls=%async_computation.3 | async-start | bytes 4194304 | tf_op jit(solution)/shard_map/all_to_all | solution.py:157
  29.3 4.2 reshape.284
  33.5 39.0 %all-to-all-done.3 = bf16[16,4,8,2048]{3,2,1,0:T(8,128)(2,1)S(1)} async-done(((bf16[16,4,8,2048]{3,2,1,0:T(8,128)(2,1)}), bf16[16,4,8,2048]{3,2,1,0:T(8,128)(2,1)S(1)}, u32[]{:S(2)}, u32[]{:S(2)}) %all-to-all-start.3) | async-done | bytes 2097184 | tf_op jit(solution)/shard_map/all_to_all | solution.py:157
  72.5 5.4 all-to-all-start.2
  82.2 4.2 reshape.280
  86.4 38.7 %all-to-all-done.2 = bf16[16,4,8,2048]{3,2,1,0:T(8,128)(2,1)} async-done(((bf16[16,4,8,2048]{3,2,1,0:T(8,128)(2,1)}), bf16[16,4,8,2048]{3,2,1,0:T(8,128)(2,1)}, u32[]{:S(2)}, u32[]{:S(2)}) %all-to-all-start.2) | async-done | bytes 2097184 | tf_op jit(solution)/shard_map/all_to_all | solution.py:156
  125.1 5.1 all-to-all-start
  147.0 30.7 %all-to-all-done = bf16[16,4,8,2048]{3,2,1,0:T(8,128)(2,1)} async-done(((bf16[16,4,8,2048]{3,2,1,0:T(8,128)(2,1)}), bf16[16,4,8,2048]{3,2,1,0:T(8,128)(2,1)}, u32[]{:S(2)}, u32[]{:S(2)}) %all-to-all-start) | async-done | bytes 2097184 | tf_op jit(solution)/shard_map/all_to_all | solution.py:158
  180.0 21.8 %fusion.119 = (f32[16,4,16,8]{3,2,1,0:T(8,128)}, f32[16,4,16,8,16,8]{4,3,5,2,1,0:T(8,128)}) fusion(bf16[16,4,8,16,128,1]{4,3,2,1,0,5:T(8,128)(2,1)} %bitcast.229, bf16[16,4,8,16,128,1]{4,3,2,1,0,5:T(8,128)(2,1)} %bitcast.215, pred[16,8,16,8]{2,1,3,0:T(8,128)(4,1)S(1)} %copy-done.28, pred[16,8,16,8]{2,1,3,0:T(8,128)(4,1)S(1)} %get-tuple-element.92, ...), kind=kOutput, calls=%fused_computation.139 | convolution fusion | flops 273670144 | bytes 8462336 | tf_op jit(solution)/shard_map/scahd,tcbhd->hcsatb/dot_general | solution.py:41
  201.8 16.3 %exponential_reduce_fusion = f32[16,4,16,8]{3,2,1,0:T(8,128)S(1)} fusion(f32[16,4,16,8,16,8]{4,3,5,2,1,0:T(8,128)} %get-tuple-element.99, f32[16,4,16,8]{3,2,1,0:T(8,128)} %get-tuple-element.98), kind=kLoop, calls=%fused_computation.2 | loop fusion | flops 2088960 | bytes 4259840 | tf_op jit(solution)/shard_map/reduce_sum | solution.py:33
  218.2 4.2 copy-done.2
  222.3 8.6 %fusion = bf16[16,4,16,8,16,8]{4,3,5,2,1,0:T(8,128)(2,1)} fusion(f32[16,4,16,8,16,8]{4,3,5,2,1,0:T(8,128)S(1)} %copy-done.2, f32[16,4,16,8]{3,2,1,0:T(8,128)S(1)} %log_add_fusion), kind=kLoop, calls=%fused_computation.4 | loop fusion | flops 2097152 | bytes 6324224 | tf_op jit(solution)/shard_map/convert_element_type | solution.py:50
  230.9 20.6 %fusion.63 = bf16[16,4,8,16,128]{4,0,2,3,1:T(8,128)(2,1)S(1)} fusion(bf16[16,4,16,8,16,8]{4,3,5,2,1,0:T(8,128)(2,1)} %fusion, bf16[16,4,8,16,128,1]{4,3,2,1,0,5:T(8,128)(2,1)S(1)} %bitcast.209), kind=kOutput, calls=%fused_computation.92 | convolution fusion | flops 269484032 | bytes 6291456 | tf_op jit(solution)/shard_map/hcsatb,tcbhd->scahd/dot_general | solution.py:52
  256.5 10.3 %all-to-all-start.4 = ((bf16[16,4,8,2048]{3,2,1,0:T(8,128)(2,1)}), bf16[16,4,8,2048]{3,2,1,0:T(8,128)(2,1)}, u32[]{:S(2)}, u32[]{:S(2)}) async-start(bf16[16,4,8,2048]{3,2,1,0:T(8,128)(2,1)} %reshape.289), calls=%async_computation.4 | async-start | bytes 4194304 | tf_op jit(solution)/shard_map/all_to_all | solution.py:164
  284.4 27.7 %all-to-all-done.4 = bf16[16,4,8,2048]{3,2,1,0:T(8,128)(2,1)} async-done(((bf16[16,4,8,2048]{3,2,1,0:T(8,128)(2,1)}), bf16[16,4,8,2048]{3,2,1,0:T(8,128)(2,1)}, u32[]{:S(2)}, u32[]{:S(2)}) %all-to-all-start.4) | async-done | bytes 2097184 | tf_op jit(solution)/shard_map/all_to_all | solution.py:164
  325.8 5.1 subtract_convert_fusion
  340.5 52.9 %all_to_all.45 = bf16[16,4,8,2048]{3,2,1,0:T(8,128)(2,1)S(1)} all-to-all(bf16[16,4,8,2048]{3,2,1,0:T(8,128)(2,1)} %reshape.298), channel_id=1, replica_groups=mesh['seq'=16,'head'=2] {'seq'}, dimensions={0} | all-to-all | bytes 4194304 | tf_op jit(solution)/shard_map/all_to_all | solution.py:212
  396.3 8.1 %fusion.73 = bf16[16,4,8,16,128]{4,0,2,3,1:T(8,128)(2,1)S(1)} fusion(bf16[16,4,16,8,16,8]{4,3,5,2,1,0:T(8,128)(2,1)} %fusion, bf16[16,4,8,16,128,1]{4,3,2,1,0,5:T(8,128)(2,1)S(1)} %bitcast.204), kind=kOutput, calls=%fused_computation.94 | convolution fusion | flops 269484032 | bytes 6291456 | tf_op jit(solution)/shard_map/hcsatb,scahd->tcbhd/dot_general | solution.py:76
  407.2 4.2 reshape.306
  411.3 6.8 %all-to-all-start.8 = ((bf16[16,4,8,2048]{3,2,1,0:T(8,128)(2,1)}), bf16[16,4,8,2048]{3,2,1,0:T(8,128)(2,1)}, u32[]{:S(2)}, u32[]{:S(2)}) async-start(bf16[16,4,8,2048]{3,2,1,0:T(8,128)(2,1)} %reshape.306), calls=%async_computation.8 | async-start | bytes 4194304 | tf_op jit(solution)/shard_map/all_to_all | solution.py:226
  418.4 29.2 %multiply_convert_fusion = bf16[16,4,16,8,16,8]{4,3,5,2,1,0:T(8,128)(2,1)} fusion(f32[16,4,16,8,16,8]{4,3,5,2,1,0:T(8,128)} %get-tuple-element.99, f32[16,4,16,8]{3,2,1,0:T(8,128)S(1)} %copy.232, f32[16,4,16,8]{3,2,1,0:T(8,128)S(1)} %copy-done.13, bf16[16,4,8,16,128,1]{4,3,2,1,0,5:T(8,128)(2,1)} %bitcast.210, bf16[16,4,8,16,128,1]{4,3,2,1,0,5:T(8,128)(2,1)S(1)} %bitcast.205), kind=kOutput, calls=%fused_computation | convolution fusion | flops 272629760 | bytes 10551296 | tf_op jit(solution)/shard_map/scahd,tcbhd->hcsatb/dot_general | solution.py:69
  447.6 8.1 %fusion.68 = bf16[16,4,8,16,128]{4,0,2,3,1:T(8,128)(2,1)S(1)} fusion(bf16[16,4,16,8,16,8]{4,3,5,2,1,0:T(8,128)(2,1)} %multiply_convert_fusion, bf16[16,4,8,16,128,1]{4,3,2,1,0,5:T(8,128)(2,1)S(1)} %bitcast.216), kind=kOutput, calls=%fused_computation.93 | convolution fusion | flops 270532608 | bytes 6291456 | tf_op jit(solution)/shard_map/hcsatb,scahd->tcbhd/dot_general | solution.py:75
  459.4 5.6 all-to-all-done.8
  465.0 5.1 all-to-all-start.7
  472.3 7.8 %convolution_bitcast_fusion = f32[512,16,128]{0,2,1:T(8,128)} fusion(bf16[256,16,128]{0,2,1:T(8,128)(2,1)S(1)} %bitcast.213, f32[16,512,256]{2,1,0:T(8,128)} %copy-done.3, f32[16,256]{1,0:T(8,128)S(1)} %log_add_fusion.1, pred[256,512]{0,1:T(8,128)(4,1)S(1)} %fusion.104), kind=kOutput, calls=%fused_computation.46 | convolution fusion | flops 545259520 | bytes 13778944 | tf_op jit(solution)/shard_map/hij,ihd->jhd/dot_general | solution.py:197
  480.1 4.3 multiply_convert_fusion.1
  484.5 20.9 %fusion.58 = bf16[16,4,8,16,128]{4,0,2,3,1:T(8,128)(2,1)S(1)} fusion(bf16[16,4,16,8,16,8]{4,3,5,2,1,0:T(8,128)(2,1)} %multiply_convert_fusion, bf16[16,4,8,16,128,1]{4,3,2,1,0,5:T(8,128)(2,1)S(1)} %bitcast.230), kind=kOutput, calls=%fused_computation.91 | convolution fusion | flops 270532608 | bytes 6291456 | tf_op jit(solution)/shard_map/hcsatb,tcbhd->scahd/dot_general | solution.py:74
  509.1 8.3 %all-to-all-done.7 = bf16[16,4,8,2048]{3,2,1,0:T(8,128)(2,1)} async-done(((bf16[16,4,8,2048]{3,2,1,0:T(8,128)(2,1)}), bf16[16,4,8,2048]{3,2,1,0:T(8,128)(2,1)}, u32[]{:S(2)}, u32[]{:S(2)}) %all-to-all-start.7) | async-done | bytes 2097184 | tf_op jit(solution)/shard_map/all_to_all | solution.py:225
  517.5 5.4 all-to-all-start.6
  522.9 3.7 convolution_bitcast_fusion.1
  547.0 66.9 %collective-permute-done.1 = bf16[2,256,2048]{2,1,0:T(8,128)(2,1)} collective-permute-done((bf16[2,256,2048]{2,1,0:T(8,128)(2,1)}, bf16[2,256,2048]{2,1,0:T(8,128)(2,1)}, u32[]{:S(2)}, u32[]{:S(2)}) %collective-permute-start.1) | collective-permute-done | bytes 2097184 | tf_op jit(solution)/shard_map/ppermute | solution.py:17
  (164 shorter events, 140.8 us)
Async XLA Ops:
  0.6 12.1 %copy-start = (bf16[256,2048]{1,0:T(8,128)(2,1)S(1)}, bf16[256,2048]{1,0:T(8,128)(2,1)}, u32[]{:S(2)}) copy-start(bf16[256,2048]{1,0:T(8,128)(2,1)} %param.23) | copy-start | bytes 3145732
  3.6 328.0 %copy-start.29 = (s32[16,256]{1,0:T(8,128)}, s32[16,256]{1,0:T(8,128)S(1)}, u32[]{:S(2)}) copy-start(s32[16,256]{1,0:T(8,128)S(1)} %multiply_add_fusion) | copy-start | bytes 49156
  5.6 12.4 %all-to-all-start.1 = ((bf16[16,2,256]{2,1,0:T(2,128)(2,1)}), bf16[16,2,256]{2,1,0:T(2,128)(2,1)S(1)}, u32[]{:S(2)}, u32[]{:S(2)}) async-start(bf16[16,2,256]{2,1,0:T(2,128)(2,1)} %reshape.323), calls=%async_computation.1 | async-start | bytes 32768 | tf_op jit(solution)/shard_map/all_to_all | solution.py:159
  18.0 7.1 %copy-start.33 = (bf16[256,2048]{1,0:T(8,128)(2,1)S(1)}, bf16[256,2048]{1,0:T(8,128)(2,1)}, u32[]{:S(2)}) copy-start(bf16[256,2048]{1,0:T(8,128)(2,1)} %param.22) | copy-start | bytes 3145732
  18.0 54.5 %all-to-all-start.3 = ((bf16[16,4,8,2048]{3,2,1,0:T(8,128)(2,1)}), bf16[16,4,8,2048]{3,2,1,0:T(8,128)(2,1)S(1)}, u32[]{:S(2)}, u32[]{:S(2)}) async-start(bf16[16,4,8,2048]{3,2,1,0:T(8,128)(2,1)} %reshape.287), calls=%async_computation.3 | async-start | bytes 4194304 | tf_op jit(solution)/shard_map/all_to_all | solution.py:157
  33.5 44.4 %copy-start.34 = (bf16[256,2048]{1,0:T(8,128)(2,1)S(1)}, bf16[256,2048]{1,0:T(8,128)(2,1)}, u32[]{:S(2)}) copy-start(bf16[256,2048]{1,0:T(8,128)(2,1)} %param.24) | copy-start | bytes 3145732
  72.5 52.6 %all-to-all-start.2 = ((bf16[16,4,8,2048]{3,2,1,0:T(8,128)(2,1)}), bf16[16,4,8,2048]{3,2,1,0:T(8,128)(2,1)}, u32[]{:S(2)}, u32[]{:S(2)}) async-start(bf16[16,4,8,2048]{3,2,1,0:T(8,128)(2,1)} %reshape.284), calls=%async_computation.2 | async-start | bytes 4194304 | tf_op jit(solution)/shard_map/all_to_all | solution.py:156
  125.1 52.6 %all-to-all-start = ((bf16[16,4,8,2048]{3,2,1,0:T(8,128)(2,1)}), bf16[16,4,8,2048]{3,2,1,0:T(8,128)(2,1)}, u32[]{:S(2)}, u32[]{:S(2)}) async-start(bf16[16,4,8,2048]{3,2,1,0:T(8,128)(2,1)} %reshape.280), calls=%async_computation | async-start | bytes 4194304 | tf_op jit(solution)/shard_map/all_to_all | solution.py:158
  136.7 132.1 %collective-permute-start = (bf16[2,256,2048]{1,2,0:T(8,128)(2,1)}, bf16[2,256,2048]{1,2,0:T(8,128)(2,1)}, u32[]{:S(2)}, u32[]{:S(2)}) collective-permute-start(bf16[2,256,2048]{1,2,0:T(8,128)(2,1)} %pad_maximum_fusion), channel_id=1, source_target_pairs={{0,2},{2,4},{4,6},{6,8},{8,10},{10,12},{12,14},{14,16},{16,18},{18... | collective-permute-start | bytes 6291464 | tf_op jit(solution)/shard_map/ppermute | solution.py:17
  179.9 51.0 %copy-start.6 = (bf16[64,8,16,128]{3,2,1,0:T(8,128)(2,1)}, bf16[64,8,16,128]{3,2,1,0:T(8,128)(2,1)S(1)}, u32[]{:S(2)}) copy-start(bf16[64,8,16,128]{3,2,1,0:T(8,128)(2,1)S(1)} %copy.290) | copy-start | bytes 6291460
  201.8 16.3 %copy-start.20 = (f32[16,4,16,8]{3,2,1,0:T(8,128)S(1)}, f32[16,4,16,8]{3,2,1,0:T(8,128)}, u32[]{:S(2)}) copy-start(f32[16,4,16,8]{3,2,1,0:T(8,128)} %get-tuple-element.98) | copy-start | bytes 98308
  201.8 20.6 %copy-start.2 = (f32[16,4,16,8,16,8]{4,3,5,2,1,0:T(8,128)S(1)}, f32[16,4,16,8,16,8]{4,3,5,2,1,0:T(8,128)}, u32[]{:S(2)}) copy-start(f32[16,4,16,8,16,8]{4,3,5,2,1,0:T(8,128)} %get-tuple-element.99) | copy-start | bytes 12582916
  222.3 8.6 %copy-start.12 = (f32[16,4,16,8]{3,2,1,0:T(8,128)}, f32[16,4,16,8]{3,2,1,0:T(8,128)S(1)}, u32[]{:S(2)}) copy-start(f32[16,4,16,8]{3,2,1,0:T(8,128)S(1)} %log_add_fusion) | copy-start | bytes 98308
  256.5 55.6 %all-to-all-start.4 = ((bf16[16,4,8,2048]{3,2,1,0:T(8,128)(2,1)}), bf16[16,4,8,2048]{3,2,1,0:T(8,128)(2,1)}, u32[]{:S(2)}, u32[]{:S(2)}) async-start(bf16[16,4,8,2048]{3,2,1,0:T(8,128)(2,1)} %reshape.289), calls=%async_computation.4 | async-start | bytes 4194304 | tf_op jit(solution)/shard_map/all_to_all | solution.py:164
  268.1 4.9 copy-start.23
  268.6 4.3 copy-start.14
  275.4 3.5 copy-start.3
  411.3 7.1 %copy-start.13 = (f32[16,4,16,8]{3,2,1,0:T(8,128)S(1)}, f32[16,4,16,8]{3,2,1,0:T(8,128)}, u32[]{:S(2)}) copy-start(f32[16,4,16,8]{3,2,1,0:T(8,128)} %copy-done.12) | copy-start | bytes 98308
  411.3 53.7 %all-to-all-start.8 = ((bf16[16,4,8,2048]{3,2,1,0:T(8,128)(2,1)}), bf16[16,4,8,2048]{3,2,1,0:T(8,128)(2,1)}, u32[]{:S(2)}, u32[]{:S(2)}) async-start(bf16[16,4,8,2048]{3,2,1,0:T(8,128)(2,1)} %reshape.306), calls=%async_computation.8 | async-start | bytes 4194304 | tf_op jit(solution)/shard_map/all_to_all | solution.py:226
  418.4 29.2 %copy-start.7 = (bf16[64,8,16,128]{3,2,1,0:T(8,128)(2,1)S(1)}, bf16[64,8,16,128]{3,2,1,0:T(8,128)(2,1)}, u32[]{:S(2)}) copy-start(bf16[64,8,16,128]{3,2,1,0:T(8,128)(2,1)} %copy.291) | copy-start | bytes 6291460
  465.0 52.5 %all-to-all-start.7 = ((bf16[16,4,8,2048]{3,2,1,0:T(8,128)(2,1)}), bf16[16,4,8,2048]{3,2,1,0:T(8,128)(2,1)}, u32[]{:S(2)}, u32[]{:S(2)}) async-start(bf16[16,4,8,2048]{3,2,1,0:T(8,128)(2,1)} %reshape.303), calls=%async_computation.7 | async-start | bytes 4194304 | tf_op jit(solution)/shard_map/all_to_all | solution.py:225
  472.0 8.1 %slice-start = ((s8[8388608]{0:T(1024)(128)(4,1)}), s8[4194304]{0:T(1024)(128)(4,1)S(1)}, s32[]{:S(2)}) async-start(s8[8388608]{0:T(1024)(128)(4,1)} %bitcast.206), calls=%async_computation.9 | async-start | bytes 8388608
  472.3 7.8 %slice-start.1 = ((s8[8388608]{0:T(1024)(128)(4,1)}), s8[4194304]{0:T(1024)(128)(4,1)S(1)}, s32[]{:S(2)}) async-start(s8[8388608]{0:T(1024)(128)(4,1)} %bitcast.206), calls=%async_computation.10 | async-start | bytes 8388608
  472.3 7.8 %copy-start.19 = (bf16[256,2048]{0,1:T(8,128)(2,1)S(1)}, bf16[256,2048]{0,1:T(8,128)(2,1)}, u32[]{:S(2)}) copy-start(bf16[256,2048]{0,1:T(8,128)(2,1)} %copy.186) | copy-start | bytes 3145732
  472.3 7.8 %copy-start.27 = (bf16[1,256,2048]{1,2,0:T(8,128)(2,1)S(1)}, bf16[1,256,2048]{1,2,0:T(8,128)(2,1)}, u32[]{:S(2)}) copy-start(bf16[1,256,2048]{1,2,0:T(8,128)(2,1)} %get-tuple-element.91) | copy-start | bytes 3145732
  480.1 4.3 copy-start.21
  509.1 13.8 %copy-start.15 = (bf16[256,2048]{0,1:T(8,128)(2,1)S(1)}, bf16[256,2048]{0,1:T(8,128)(2,1)}, u32[]{:S(2)}) copy-start(bf16[256,2048]{0,1:T(8,128)(2,1)} %copy-done.14) | copy-start | bytes 3145732
  517.5 112.3 %all-to-all-start.6 = ((bf16[16,4,8,2048]{3,2,1,0:T(8,128)(2,1)}), bf16[16,4,8,2048]{3,2,1,0:T(8,128)(2,1)}, u32[]{:S(2)}, u32[]{:S(2)}) async-start(bf16[16,4,8,2048]{3,2,1,0:T(8,128)(2,1)} %reshape.300), calls=%async_computation.6 | async-start | bytes 4194304 | tf_op jit(solution)/shard_map/all_to_all | solution.py:224
  531.8 5.9 copy-start.24
  531.8 5.9 copy-start.25
  533.3 80.6 %collective-permute-start.1 = (bf16[2,256,2048]{2,1,0:T(8,128)(2,1)}, bf16[2,256,2048]{2,1,0:T(8,128)(2,1)}, u32[]{:S(2)}, u32[]{:S(2)}) collective-permute-start(bf16[2,256,2048]{2,1,0:T(8,128)(2,1)} %pad_maximum_fusion.3), channel_id=1, source_target_pairs={{2,0},{4,2},{6,4},{8,6},{10,8},{12,10},{14,12},{16,14},{18,16},{20... | collective-permute-start | bytes 6291464 | tf_op jit(solution)/shard_map/ppermute | solution.py:17
  547.0 69.0 %copy-start.8 = (f32[256,2048]{1,0:T(8,128)S(1)}, f32[256,2048]{1,0:T(8,128)}, u32[]{:S(2)}) copy-start(f32[256,2048]{1,0:T(8,128)} %copy.224) | copy-start | bytes 6291460
  (16 other events, 40.3 us)
where the time goes:
time: 644 us; the launch traced here: 636 us
  waiting for transfers between devices  217 us (34%)
  matrix products  150 us (23%)
  local copies, waits for them, and re-layouts  104 us (16%)
  starting transfers between devices  58.5 us (9%)
  blocking collectives  55.3 us (9%)
  other arithmetic  49.6 us (8%)
    ppermute x2, waiting for transfers between devices, from_behind(): return lax.ppermute(block, axis, route)  66.9 us
    all_to_all x1, blocking collectives, body(): lax.all_to_all(grad_sent, 'seq', split_axis=0, concat_axis=0, tiled=True)  52.9 us
    unnamed x89, local copies, waits for them, and re-layouts  40.4 us
    all_to_all x1, waiting for transfers between devices, body(): lax.all_to_all(sent_key, 'seq', split_axis=0, concat_axis=0, tiled=True)  39 us
    all_to_all x1, waiting for transfers between devices, body(): lax.all_to_all(sent_query, 'seq', split_axis=0, concat_axis=0, tiled=True)  38.7 us
    all_to_all x1, waiting for transfers between devices, body(): lax.all_to_all(sent_value, 'seq', split_axis=0, concat_axis=0, tiled=True)  30.7 us
    dot_general x1, matrix products, owner_gradients(): jnp.einsum('scahd,tcbhd->hcsatb', grad_rows, val_rows, preferred_element_...  29.2 us
    all_to_all x1, waiting for transfers between devices, body(): lax.all_to_all(outputs.reshape(queries.shape), 'seq', split_axis=0, conca...  27.7 us
  transfers between devices with their start and end apart: 10, of which 7 were waited for; matrix products, arithmetic and copies ran while one was open for 37% of the time, Pallas kernels for 0%

commit v1 on v0

--- a/solution.py
+++ b/solution.py
@@ -9,6 +9,29 @@
 WINDOW = 256
 SLOTS = 128
 EPSILON = 1e-06
+
+
+def in_blocks(x, dim, size):
+    lengths = x.shape
+    blocks = x.reshape(*lengths[:dim], size, lengths[dim] // size, *lengths[dim + 1 :])
+    return jnp.moveaxis(blocks, dim, 0)
+
+
+def joined_along(pieces, dim):
+    shape = list(pieces.shape[1:])
+    shape[dim] *= pieces.shape[0]
+    return jnp.moveaxis(pieces, 0, dim).reshape(shape)
+
+
+def exchange_in_pairs(x, axis, split_dim, concat_dim):
+    size, index = (lax.axis_size(axis), lax.axis_index(axis))
+    parts = in_blocks(x, split_dim, size)
+    outs = [parts[index]]
+    for step in range(1, size):
+        sent = parts[index ^ step]
+        outs.append(lax.ppermute(sent, axis, [(i, i ^ step) for i in range(size)]))
+    parts = jnp.stack(outs)[index ^ jnp.arange(size)]
+    return joined_along(parts, concat_dim)
 
 
 def from_behind(block, axis, distance):
@@ -161,9 +184,7 @@
     k_five = five_dims(key_rows)
     v_five = five_dims(val_rows)
     attn_prob, weights, outputs = owner_attend(q_five, k_five, v_five, live_rows, factor)
-    returned = lax.all_to_all(
-        outputs.reshape(queries.shape), "seq", split_axis=0, concat_axis=0, tiled=True
-    )
+    returned = exchange_in_pairs(outputs.reshape(queries.shape), "seq", 0, 0)
     result = (returned, q_five, k_five, v_five, attn_prob, weights, outputs)
     returned = result[0]
     attn_clu = collect(returned)

time: 644 us -> 739 us (1.15)
  waiting for transfers between devices: 217 us -> 249 us
  starting transfers between devices: 58.5 us -> 89.7 us
  local copies, waits for them, and re-layouts: 104 us -> 126 us
    ppermute x2, waiting for transfers between devices: 66.9 us -> 118 us  [from_behind(): return lax.ppermute(block, axis, route)]
    ppermute x0 -> x15, starting transfers between devices: none -> 37.2 us  [exchange_in_pairs(): outs.append(lax.ppermute(sent, axis, [(i, i ^ step) for i in range(size)]))]
    ppermute x0 -> x15, waiting for transfers between devices: none -> 36.1 us  [exchange_in_pairs(): outs.append(lax.ppermute(sent, axis, [(i, i ^ step) for i in range(size)]))]
    all_to_all x1 -> x0, waiting for transfers between devices: 27.7 us -> none  [body(): lax.all_to_all(outputs.reshape(queries.shape), 'seq', split_axis=0, conca...]
    all_to_all x1, waiting for transfers between devices: 30.7 us -> 15.3 us  [body(): lax.all_to_all(sent_value, 'seq', split_axis=0, concat_axis=0, tiled=True)]
    all_to_all x1 -> x0, starting transfers between devices: 10.3 us -> none  [body(): lax.all_to_all(outputs.reshape(queries.shape), 'seq', split_axis=0, conca...]
    unnamed x89 -> x93, local copies, waits for them, and re-layouts: 40.4 us -> 50.7 us
    all_to_all x1, waiting for transfers between devices: 38.7 us -> 28.5 us  [body(): lax.all_to_all(sent_query, 'seq', split_axis=0, concat_axis=0, tiled=True)]
  transfers between devices with their start and end apart: 10 -> 24, of which waited for: 7 -> 17; matrix products, arithmetic and copies ran while one was open for 37% -> 25% of each run, Pallas kernels for 0% -> 0%
where the time goes in v1:
time: 739 us; the launch traced here: 730 us
  waiting for transfers between devices  249 us (34%)
  matrix products  156 us (21%)
  local copies, waits for them, and re-layouts  126 us (17%)
  starting transfers between devices  89.7 us (12%)
  blocking collectives  57.6 us (8%)
  other arithmetic  50.8 us (7%)
    ppermute x2, waiting for transfers between devices, from_behind(): return lax.ppermute(block, axis, route)  118 us
    all_to_all x1, blocking collectives, body(): lax.all_to_all(grad_sent, 'seq', split_axis=0, concat_axis=0, tiled=True)  55.1 us
    unnamed x93, local copies, waits for them, and re-layouts  50.7 us
    all_to_all x1, waiting for transfers between devices, body(): lax.all_to_all(sent_key, 'seq', split_axis=0, concat_axis=0, tiled=True)  39 us
    ppermute x15, starting transfers between devices, exchange_in_pairs(): outs.append(lax.ppermute(sent, axis, [(i, i ^ step) for i in range(size)]))  37.2 us
    ppermute x15, waiting for transfers between devices, exchange_in_pairs(): outs.append(lax.ppermute(sent, axis, [(i, i ^ step) for i in range(size)]))  36.1 us
    dot_general x1, matrix products, owner_gradients(): jnp.einsum('scahd,tcbhd->hcsatb', grad_rows, val_rows, preferred_element_...  29.3 us
    all_to_all x1, waiting for transfers between devices, body(): lax.all_to_all(sent_query, 'seq', split_axis=0, concat_axis=0, tiled=True)  28.5 us
  transfers between devices with their start and end apart: 24, of which 17 were waited for; matrix products, arithmetic and copies ran while one was open for 25% of the time, Pallas kernels for 0%

profile of v1, /device:TPU:14, one launch (start us, length us, event | category | flops | bytes accessed | tf_op | source)
XLA Modules:
  0.0 730.0 jit_solution(15068404659767829096)
XLA Ops:
  5.6 7.1 all-to-all-start.1
  18.0 7.0 all-to-all-start.3
  33.5 39.0 %all-to-all-done.3 = bf16[16,4,8,2048]{3,2,1,0:T(8,128)(2,1)S(1)} async-done(((bf16[16,4,8,2048]{3,2,1,0:T(8,128)(2,1)}), bf16[16,4,8,2048]{3,2,1,0:T(8,128)(2,1)S(1)}, u32[]{:S(2)}, u32[]{:S(2)}) %all-to-all-start.3) | async-done | bytes 2097184 | tf_op jit(solution)/shard_map/all_to_all | solution.py:180
  72.5 5.1 all-to-all-start.2
  96.6 28.5 %all-to-all-done.2 = bf16[16,4,8,2048]{3,2,1,0:T(8,128)(2,1)} async-done(((bf16[16,4,8,2048]{3,2,1,0:T(8,128)(2,1)}), bf16[16,4,8,2048]{3,2,1,0:T(8,128)(2,1)}, u32[]{:S(2)}, u32[]{:S(2)}) %all-to-all-start.2) | async-done | bytes 2097184 | tf_op jit(solution)/shard_map/all_to_all | solution.py:179
  125.1 9.8 %all-to-all-start = ((bf16[16,4,8,2048]{3,2,1,0:T(8,128)(2,1)}), bf16[16,4,8,2048]{3,2,1,0:T(8,128)(2,1)}, u32[]{:S(2)}, u32[]{:S(2)}) async-start(bf16[16,4,8,2048]{3,2,1,0:T(8,128)(2,1)} %reshape.290), calls=%async_computation | async-start | bytes 4194304 | tf_op jit(solution)/shard_map/all_to_all | solution.py:181
  140.2 51.4 %collective-permute-done = bf16[2,256,2048]{1,2,0:T(8,128)(2,1)} collective-permute-done((bf16[2,256,2048]{1,2,0:T(8,128)(2,1)}, bf16[2,256,2048]{1,2,0:T(8,128)(2,1)}, u32[]{:S(2)}, u32[]{:S(2)}) %collective-permute-start) | collective-permute-done | bytes 2097184 | tf_op jit(solution)/shard_map/ppermute | solution.py:40
  208.6 15.3 %all-to-all-done = bf16[16,4,8,2048]{3,2,1,0:T(8,128)(2,1)} async-done(((bf16[16,4,8,2048]{3,2,1,0:T(8,128)(2,1)}), bf16[16,4,8,2048]{3,2,1,0:T(8,128)(2,1)}, u32[]{:S(2)}, u32[]{:S(2)}) %all-to-all-start) | async-done | bytes 2097184 | tf_op jit(solution)/shard_map/all_to_all | solution.py:181
  226.2 21.0 %fusion.120 = (f32[16,4,16,8]{3,2,1,0:T(8,128)S(1)}, f32[16,4,16,8,16,8]{4,3,5,2,1,0:T(8,128)}) fusion(bf16[16,4,8,16,128,1]{4,3,2,1,0,5:T(8,128)(2,1)} %bitcast.292, bf16[16,4,8,16,128,1]{4,3,2,1,0,5:T(8,128)(2,1)} %bitcast.276, pred[16,8,16,8]{2,1,3,0:T(8,128)(4,1)S(1)} %copy-done.23, pred[16,8,16,8]{2,1,3,0:T(8,128)(4,1)S(1)} %copy-done.22, ...), kind=kOutput, calls=%fused_computation.174 | convolution fusion | flops 273670144 | bytes 8462336 | tf_op jit(solution)/shard_map/scahd,tcbhd->hcsatb/dot_general | solution.py:64
  247.1 16.0 %exponential_reduce_fusion = f32[16,4,16,8]{3,2,1,0:T(8,128)S(1)} fusion(f32[16,4,16,8,16,8]{4,3,5,2,1,0:T(8,128)} %get-tuple-element.115, f32[16,4,16,8]{3,2,1,0:T(8,128)S(1)} %get-tuple-element.114), kind=kLoop, calls=%fused_computation.3 | loop fusion | flops 2088960 | bytes 4259840 | tf_op jit(solution)/shard_map/reduce_sum | solution.py:56
  267.4 8.6 %fusion = bf16[16,4,16,8,16,8]{4,3,5,2,1,0:T(8,128)(2,1)} fusion(f32[16,4,16,8,16,8]{4,3,5,2,1,0:T(8,128)S(1)} %copy-done.2, f32[16,4,16,8]{3,2,1,0:T(8,128)S(1)} %log_add_fusion), kind=kLoop, calls=%fused_computation.5 | loop fusion | flops 2097152 | bytes 6324224 | tf_op jit(solution)/shard_map/convert_element_type | solution.py:73
  276.0 20.6 %fusion.63 = bf16[16,4,8,16,128]{4,0,2,3,1:T(8,128)(2,1)S(1)} fusion(bf16[16,4,16,8,16,8]{4,3,5,2,1,0:T(8,128)(2,1)} %fusion, bf16[16,4,8,16,128,1]{4,3,2,1,0,5:T(8,128)(2,1)S(1)} %bitcast.270), kind=kOutput, calls=%fused_computation.93 | convolution fusion | flops 269484032 | bytes 6291456 | tf_op jit(solution)/shard_map/hcsatb,tcbhd->scahd/dot_general | solution.py:75
  305.9 7.5 %fusion.53 = (f32[256]{0:T(256)}, f32[16,128,256]{2,1,0:T(8,128)}) fusion(f32[16,512,256]{2,1,0:T(8,128)} %copy-done.3, f32[16,256]{1,0:T(8,128)S(1)} %log_add_fusion.1, pred[256,512]{0,1:T(8,128)(4,1)S(1)} %fusion.104, bf16[256,16,128]{0,2,1:T(8,128)(2,1)S(1)} %bitcast.288, bf16[256,16,128]{0,2,1:T(8,128)(2,1)S(1)} %bitcast.305), kind=kOutput, calls=%fused_computation.73 | convolution fusion | flops 551550720 | bytes 12731392 | tf_op jit(solution)/shard_map/hij,jhd->ihd/dot_general | solution.py:148
  340.9 6.5 collective-permute-start.5
  353.2 4.6 collective-permute-done.6
  361.2 4.8 collective-permute-done.7
  366.9 6.2 collective-permute-done.8
  388.4 4.8 collective-permute-start.11
  417.1 5.4 subtract_convert_fusion
  433.0 55.1 %all_to_all.40 = bf16[16,4,8,2048]{3,2,1,0:T(8,128)(2,1)S(1)} all-to-all(bf16[16,4,8,2048]{3,2,1,0:T(8,128)(2,1)} %reshape.306), channel_id=1, replica_groups=mesh['seq'=16,'head'=2] {'seq'}, dimensions={0} | all-to-all | bytes 4194304 | tf_op jit(solution)/shard_map/all_to_all | solution.py:233
  491.1 8.1 %fusion.73 = bf16[16,4,8,16,128]{4,0,2,3,1:T(8,128)(2,1)S(1)} fusion(bf16[16,4,16,8,16,8]{4,3,5,2,1,0:T(8,128)(2,1)} %fusion, bf16[16,4,8,16,128,1]{4,3,2,1,0,5:T(8,128)(2,1)S(1)} %bitcast.267), kind=kOutput, calls=%fused_computation.95 | convolution fusion | flops 269484032 | bytes 6291456 | tf_op jit(solution)/shard_map/hcsatb,scahd->tcbhd/dot_general | solution.py:99
  506.1 6.4 all-to-all-start.7
  512.7 29.3 %multiply_convert_fusion = bf16[16,4,16,8,16,8]{4,3,5,2,1,0:T(8,128)(2,1)} fusion(f32[16,4,16,8,16,8]{4,3,5,2,1,0:T(8,128)} %get-tuple-element.115, f32[16,4,16,8]{3,2,1,0:T(8,128)S(1)} %copy.232, f32[16,4,16,8]{3,2,1,0:T(8,128)S(1)} %log_add_fusion, bf16[16,4,8,16,128,1]{4,3,2,1,0,5:T(8,128)(2,1)} %bitcast.271, ...), kind=kOutput, calls=%fused_computation.1 | convolution fusion | flops 272629760 | bytes 10551296 | tf_op jit(solution)/shard_map/scahd,tcbhd->hcsatb/dot_general | solution.py:92
  542.0 8.1 %fusion.68 = bf16[16,4,8,16,128]{4,0,2,3,1:T(8,128)(2,1)S(1)} fusion(bf16[16,4,16,8,16,8]{4,3,5,2,1,0:T(8,128)(2,1)} %multiply_convert_fusion, bf16[16,4,8,16,128,1]{4,3,2,1,0,5:T(8,128)(2,1)S(1)} %bitcast.277), kind=kOutput, calls=%fused_computation.94 | convolution fusion | flops 270532608 | bytes 6291456 | tf_op jit(solution)/shard_map/hcsatb,scahd->tcbhd/dot_general | solution.py:98
  553.8 5.6 all-to-all-done.7
  559.4 5.1 all-to-all-start.6
  566.7 7.8 %convolution_bitcast_fusion = f32[512,16,128]{0,2,1:T(8,128)} fusion(bf16[256,16,128]{0,2,1:T(8,128)(2,1)S(1)} %bitcast.274, f32[16,512,256]{2,1,0:T(8,128)} %copy-done.3, f32[16,256]{1,0:T(8,128)S(1)} %log_add_fusion.1, pred[256,512]{0,1:T(8,128)(4,1)S(1)} %fusion.104), kind=kOutput, calls=%fused_computation.47 | convolution fusion | flops 545259520 | bytes 13778944 | tf_op jit(solution)/shard_map/hij,ihd->jhd/dot_general | solution.py:218
  574.5 6.6 multiply_convert_fusion.1
  581.1 20.9 %fusion.58 = bf16[16,4,8,16,128]{4,0,2,3,1:T(8,128)(2,1)S(1)} fusion(bf16[16,4,16,8,16,8]{4,3,5,2,1,0:T(8,128)(2,1)} %multiply_convert_fusion, bf16[16,4,8,16,128,1]{4,3,2,1,0,5:T(8,128)(2,1)S(1)} %bitcast.293), kind=kOutput, calls=%fused_computation.92 | convolution fusion | flops 270532608 | bytes 6291456 | tf_op jit(solution)/shard_map/hcsatb,tcbhd->scahd/dot_general | solution.py:97
  605.6 6.2 all-to-all-done.6
  611.9 5.4 all-to-all-start.5
  641.4 66.9 %collective-permute-done.16 = bf16[2,256,2048]{2,1,0:T(8,128)(2,1)} collective-permute-done((bf16[2,256,2048]{2,1,0:T(8,128)(2,1)}, bf16[2,256,2048]{2,1,0:T(8,128)(2,1)}, u32[]{:S(2)}, u32[]{:S(2)}) %collective-permute-start.16) | collective-permute-done | bytes 2097184 | tf_op jit(solution)/shard_map/ppermute | solution.py:40
  (200 shorter events, 227.8 us)
Async XLA Ops:
  0.6 12.1 %copy-start = (bf16[256,2048]{1,0:T(8,128)(2,1)S(1)}, bf16[256,2048]{1,0:T(8,128)(2,1)}, u32[]{:S(2)}) copy-start(bf16[256,2048]{1,0:T(8,128)(2,1)} %param.23) | copy-start | bytes 3145732
  3.6 84.6 %copy-start.24 = (s32[16,256]{1,0:T(8,128)}, s32[16,256]{1,0:T(8,128)S(1)}, u32[]{:S(2)}) copy-start(s32[16,256]{1,0:T(8,128)S(1)} %multiply_add_fusion) | copy-start | bytes 49156
  5.6 12.4 %all-to-all-start.1 = ((bf16[16,2,256]{2,1,0:T(2,128)(2,1)}), bf16[16,2,256]{2,1,0:T(2,128)(2,1)S(1)}, u32[]{:S(2)}, u32[]{:S(2)}) async-start(bf16[16,2,256]{2,1,0:T(2,128)(2,1)} %reshape.342), calls=%async_computation.1 | async-start | bytes 32768 | tf_op jit(solution)/shard_map/all_to_all | solution.py:182
  18.0 54.5 %all-to-all-start.3 = ((bf16[16,4,8,2048]{3,2,1,0:T(8,128)(2,1)}), bf16[16,4,8,2048]{3,2,1,0:T(8,128)(2,1)S(1)}, u32[]{:S(2)}, u32[]{:S(2)}) async-start(bf16[16,4,8,2048]{3,2,1,0:T(8,128)(2,1)} %reshape.297), calls=%async_computation.3 | async-start | bytes 4194304 | tf_op jit(solution)/shard_map/all_to_all | solution.py:180
  72.5 52.6 %all-to-all-start.2 = ((bf16[16,4,8,2048]{3,2,1,0:T(8,128)(2,1)}), bf16[16,4,8,2048]{3,2,1,0:T(8,128)(2,1)}, u32[]{:S(2)}, u32[]{:S(2)}) async-start(bf16[16,4,8,2048]{3,2,1,0:T(8,128)(2,1)} %reshape.294), calls=%async_computation.2 | async-start | bytes 4194304 | tf_op jit(solution)/shard_map/all_to_all | solution.py:179
  84.3 107.4 %collective-permute-start = (bf16[2,256,2048]{1,2,0:T(8,128)(2,1)}, bf16[2,256,2048]{1,2,0:T(8,128)(2,1)}, u32[]{:S(2)}, u32[]{:S(2)}) collective-permute-start(bf16[2,256,2048]{1,2,0:T(8,128)(2,1)} %pad_maximum_fusion), channel_id=1, source_target_pairs={{0,2},{2,4},{4,6},{6,8},{8,10},{10,12},{12,14},{14,16},{16,18},{18... | collective-permute-start | bytes 6291464 | tf_op jit(solution)/shard_map/ppermute | solution.py:40
  125.1 98.7 %all-to-all-start = ((bf16[16,4,8,2048]{3,2,1,0:T(8,128)(2,1)}), bf16[16,4,8,2048]{3,2,1,0:T(8,128)(2,1)}, u32[]{:S(2)}, u32[]{:S(2)}) async-start(bf16[16,4,8,2048]{3,2,1,0:T(8,128)(2,1)} %reshape.290), calls=%async_computation | async-start | bytes 4194304 | tf_op jit(solution)/shard_map/all_to_all | solution.py:181
  137.7 59.2 %copy-start.12 = (bf16[256,2048]{0,1:T(8,128)(2,1)}, bf16[256,2048]{0,1:T(8,128)(2,1)S(1)}, u32[]{:S(2)}) copy-start(bf16[256,2048]{0,1:T(8,128)(2,1)S(1)} %copy.286) | copy-start | bytes 3145732
  226.1 49.8 %copy-start.6 = (bf16[64,8,16,128]{3,2,1,0:T(8,128)(2,1)}, bf16[64,8,16,128]{3,2,1,0:T(8,128)(2,1)S(1)}, u32[]{:S(2)}) copy-start(bf16[64,8,16,128]{3,2,1,0:T(8,128)(2,1)S(1)} %copy.290) | copy-start | bytes 6291460
  247.1 20.2 %copy-start.2 = (f32[16,4,16,8,16,8]{4,3,5,2,1,0:T(8,128)S(1)}, f32[16,4,16,8,16,8]{4,3,5,2,1,0:T(8,128)}, u32[]{:S(2)}) copy-start(f32[16,4,16,8,16,8]{4,3,5,2,1,0:T(8,128)} %get-tuple-element.115) | copy-start | bytes 12582916
  305.0 16.7 %collective-permute-start.1 = (bf16[1,4,8,2048]{3,2,1,0:T(8,128)(2,1)}, bf16[1,4,8,2048]{3,2,1,0:T(8,128)(2,1)}, u32[]{:S(2)}, u32[]{:S(2)}) collective-permute-start(bf16[1,4,8,2048]{3,2,1,0:T(8,128)(2,1)} %get-tuple-element.104), channel_id=1, source_target_pairs={{0,2},{2,0},{4,6},{6,4},{8,10},{10,8},{12,14},{14,12},{16,18},{18,... | collective-permute-start | bytes 393224 | tf_op jit(solution)/shard_map/ppermute | solution.py:32
  315.3 83.4 %collective-permute-start.15 = (bf16[1,4,8,2048]{3,2,1,0:T(8,128)(2,1)S(1)}, bf16[1,4,8,2048]{3,2,1,0:T(8,128)(2,1)S(1)}, u32[]{:S(2)}, u32[]{:S(2)}) collective-permute-start(bf16[1,4,8,2048]{3,2,1,0:T(8,128)(2,1)S(1)} %get-tuple-element.90), channel_id=1, source_target_pairs={{0,30},{2,28},{4,26},{6,24},{8,22},{10,20},{12,18},{14,16},{16,14}... | collective-permute-start | bytes 393224 | tf_op jit(solution)/shard_map/ppermute | solution.py:32
  319.4 78.7 %collective-permute-start.14 = (bf16[1,4,8,2048]{3,2,1,0:T(8,128)(2,1)S(1)}, bf16[1,4,8,2048]{3,2,1,0:T(8,128)(2,1)S(1)}, u32[]{:S(2)}, u32[]{:S(2)}) collective-permute-start(bf16[1,4,8,2048]{3,2,1,0:T(8,128)(2,1)S(1)} %get-tuple-element.91), channel_id=1, source_target_pairs={{0,28},{2,30},{4,24},{6,26},{8,20},{10,22},{12,16},{14,18},{16,12}... | collective-permute-start | bytes 393224 | tf_op jit(solution)/shard_map/ppermute | solution.py:32
  319.4 78.1 %collective-permute-start.13 = (bf16[1,4,8,2048]{3,2,1,0:T(8,128)(2,1)S(1)}, bf16[1,4,8,2048]{3,2,1,0:T(8,128)(2,1)S(1)}, u32[]{:S(2)}, u32[]{:S(2)}) collective-permute-start(bf16[1,4,8,2048]{3,2,1,0:T(8,128)(2,1)S(1)} %get-tuple-element.92), channel_id=1, source_target_pairs={{0,26},{2,24},{4,30},{6,28},{8,18},{10,16},{12,22},{14,20},{16,10}... | collective-permute-start | bytes 393224 | tf_op jit(solution)/shard_map/ppermute | solution.py:32
  319.4 77.4 %collective-permute-start.12 = (bf16[1,4,8,2048]{3,2,1,0:T(8,128)(2,1)S(1)}, bf16[1,4,8,2048]{3,2,1,0:T(8,128)(2,1)S(1)}, u32[]{:S(2)}, u32[]{:S(2)}) collective-permute-start(bf16[1,4,8,2048]{3,2,1,0:T(8,128)(2,1)S(1)} %get-tuple-element.93), channel_id=1, source_target_pairs={{0,24},{2,26},{4,28},{6,30},{8,16},{10,18},{12,20},{14,22},{16,8},... | collective-permute-start | bytes 393224 | tf_op jit(solution)/shard_map/ppermute | solution.py:32
  321.7 5.2 collective-permute-start.2
  326.9 8.0 %collective-permute-start.3 = (bf16[1,4,8,2048]{3,2,1,0:T(8,128)(2,1)}, bf16[1,4,8,2048]{3,2,1,0:T(8,128)(2,1)S(1)}, u32[]{:S(2)}, u32[]{:S(2)}) collective-permute-start(bf16[1,4,8,2048]{3,2,1,0:T(8,128)(2,1)} %get-tuple-element.102), channel_id=1, source_target_pairs={{0,6},{2,4},{4,2},{6,0},{8,14},{10,12},{12,10},{14,8},{16,22},{18,... | collective-permute-start | bytes 393224 | tf_op jit(solution)/shard_map/ppermute | solution.py:32
  334.9 6.0 collective-permute-start.4
  340.9 10.4 %collective-permute-start.5 = (bf16[1,4,8,2048]{3,2,1,0:T(8,128)(2,1)}, bf16[1,4,8,2048]{3,2,1,0:T(8,128)(2,1)S(1)}, u32[]{:S(2)}, u32[]{:S(2)}) collective-permute-start(bf16[1,4,8,2048]{3,2,1,0:T(8,128)(2,1)} %get-tuple-element.100), channel_id=1, source_target_pairs={{0,10},{2,8},{4,14},{6,12},{8,2},{10,0},{12,6},{14,4},{16,26},{18,... | collective-permute-start | bytes 393224 | tf_op jit(solution)/shard_map/ppermute | solution.py:32
  351.3 6.6 collective-permute-start.6
  357.8 8.2 %collective-permute-start.7 = (bf16[1,4,8,2048]{3,2,1,0:T(8,128)(2,1)}, bf16[1,4,8,2048]{3,2,1,0:T(8,128)(2,1)S(1)}, u32[]{:S(2)}, u32[]{:S(2)}) collective-permute-start(bf16[1,4,8,2048]{3,2,1,0:T(8,128)(2,1)} %get-tuple-element.98), channel_id=1, source_target_pairs={{0,14},{2,12},{4,10},{6,8},{8,6},{10,4},{12,2},{14,0},{16,30},{18,... | collective-permute-start | bytes 393224 | tf_op jit(solution)/shard_map/ppermute | solution.py:32
  366.0 7.1 collective-permute-start.8
  373.1 7.8 %collective-permute-start.9 = (bf16[1,4,8,2048]{3,2,1,0:T(8,128)(2,1)}, bf16[1,4,8,2048]{3,2,1,0:T(8,128)(2,1)S(1)}, u32[]{:S(2)}, u32[]{:S(2)}) collective-permute-start(bf16[1,4,8,2048]{3,2,1,0:T(8,128)(2,1)} %get-tuple-element.96), channel_id=1, source_target_pairs={{0,18},{2,16},{4,22},{6,20},{8,26},{10,24},{12,30},{14,28},{16,2},... | collective-permute-start | bytes 393224 | tf_op jit(solution)/shard_map/ppermute | solution.py:32
  380.9 7.5 %collective-permute-start.10 = (bf16[1,4,8,2048]{3,2,1,0:T(8,128)(2,1)S(1)}, bf16[1,4,8,2048]{3,2,1,0:T(8,128)(2,1)S(1)}, u32[]{:S(2)}, u32[]{:S(2)}) collective-permute-start(bf16[1,4,8,2048]{3,2,1,0:T(8,128)(2,1)S(1)} %get-tuple-element.95), channel_id=1, source_target_pairs={{0,20},{2,22},{4,16},{6,18},{8,28},{10,30},{12,24},{14,26},{16,4},... | collective-permute-start | bytes 393224 | tf_op jit(solution)/shard_map/ppermute | solution.py:32
  388.4 7.7 %collective-permute-start.11 = (bf16[1,4,8,2048]{3,2,1,0:T(8,128)(2,1)S(1)}, bf16[1,4,8,2048]{3,2,1,0:T(8,128)(2,1)S(1)}, u32[]{:S(2)}, u32[]{:S(2)}) collective-permute-start(bf16[1,4,8,2048]{3,2,1,0:T(8,128)(2,1)S(1)} %get-tuple-element.94), channel_id=1, source_target_pairs={{0,22},{2,20},{4,18},{6,16},{8,30},{10,28},{12,26},{14,24},{16,6},... | collective-permute-start | bytes 393224 | tf_op jit(solution)/shard_map/ppermute | solution.py:32
  506.1 53.3 %all-to-all-start.7 = ((bf16[16,4,8,2048]{3,2,1,0:T(8,128)(2,1)}), bf16[16,4,8,2048]{3,2,1,0:T(8,128)(2,1)}, u32[]{:S(2)}, u32[]{:S(2)}) async-start(bf16[16,4,8,2048]{3,2,1,0:T(8,128)(2,1)} %reshape.314), calls=%async_computation.7 | async-start | bytes 4194304 | tf_op jit(solution)/shard_map/all_to_all | solution.py:247
  512.7 29.3 %copy-start.7 = (bf16[64,8,16,128]{3,2,1,0:T(8,128)(2,1)S(1)}, bf16[64,8,16,128]{3,2,1,0:T(8,128)(2,1)}, u32[]{:S(2)}) copy-start(bf16[64,8,16,128]{3,2,1,0:T(8,128)(2,1)} %copy.291) | copy-start | bytes 6291460
  559.4 52.5 %all-to-all-start.6 = ((bf16[16,4,8,2048]{3,2,1,0:T(8,128)(2,1)}), bf16[16,4,8,2048]{3,2,1,0:T(8,128)(2,1)}, u32[]{:S(2)}, u32[]{:S(2)}) async-start(bf16[16,4,8,2048]{3,2,1,0:T(8,128)(2,1)} %reshape.311), calls=%async_computation.6 | async-start | bytes 4194304 | tf_op jit(solution)/shard_map/all_to_all | solution.py:246
  605.6 11.7 %copy-start.13 = (bf16[256,2048]{0,1:T(8,128)(2,1)S(1)}, bf16[256,2048]{0,1:T(8,128)(2,1)}, u32[]{:S(2)}) copy-start(bf16[256,2048]{0,1:T(8,128)(2,1)} %copy-done.12) | copy-start | bytes 3145732
  611.9 112.3 %all-to-all-start.5 = ((bf16[16,4,8,2048]{3,2,1,0:T(8,128)(2,1)}), bf16[16,4,8,2048]{3,2,1,0:T(8,128)(2,1)}, u32[]{:S(2)}, u32[]{:S(2)}) async-start(bf16[16,4,8,2048]{3,2,1,0:T(8,128)(2,1)} %reshape.308), calls=%async_computation.5 | async-start | bytes 4194304 | tf_op jit(solution)/shard_map/all_to_all | solution.py:245
  627.7 80.7 %collective-permute-start.16 = (bf16[2,256,2048]{2,1,0:T(8,128)(2,1)}, bf16[2,256,2048]{2,1,0:T(8,128)(2,1)}, u32[]{:S(2)}, u32[]{:S(2)}) collective-permute-start(bf16[2,256,2048]{2,1,0:T(8,128)(2,1)} %pad_maximum_fusion.3), channel_id=1, source_target_pairs={{2,0},{4,2},{6,4},{8,6},{10,8},{12,10},{14,12},{16,14},{18,16},{20... | collective-permute-start | bytes 6291464 | tf_op jit(solution)/shard_map/ppermute | solution.py:40
  641.4 69.0 %copy-start.8 = (f32[256,2048]{1,0:T(8,128)S(1)}, f32[256,2048]{1,0:T(8,128)}, u32[]{:S(2)}) copy-start(f32[256,2048]{1,0:T(8,128)} %copy.224) | copy-start | bytes 6291460
  (25 other events, 91.0 us)
